TPU v7x, 32 devices: a whole 2x2x4 slice. The times are simulated.
32 devices in a mesh: sec: 2 (over core), elem: 16 (over z, y, x).
Axes of the slice: x: 2, y: 2, z: 4, core: 2. Of those that a mesh axis runs over, the one named last changes fastest.
Arguments:
- fields: float32 [2, 320, 16384], P('sec', None, 'elem'), may hold values from -6 to 6
- jacobian: float32 [2, 16384], P('sec', 'elem'), may hold values from 0.25 to 2.5
- face_links: int32 [2, 6, 16384], P('sec', None, 'elem'), may hold values from 0 to 1535, as said below
- volume_matrix: float32 [2, 320, 320], P('sec'), may hold values from -0.3125 to 0.3125
- face_matrices: float32 [2, 6, 320, 320], P('sec'), may hold values from -0.3125 to 0.3125
- patterns: float32 [4, 64, 64], replicated, may hold values from 0 to 0.03125
- donor_index: int32 [2, 2048], P('sec', 'elem'), may hold values from 0 to 1023
- pattern_index: int32 [2, 2048], P('sec', 'elem'), may hold values from 0 to 3
- receivers: int32 [2, 2048], P('sec', 'elem'), may hold values from -1 to 1023, as said below
Outputs:
- advanced: float32 [2, 320, 16384], P('sec', None, 'elem')
Inputs may be any that keep to these rules, and one draw needn't show every extreme that they name: face_links[s, f, g] counts from the lowest rim element of the device holding element g; index 256 is that device's first own element. receivers holds on each device 8 slots for each device of the other section, source-major; -1 marks an empty slot, other entries on one device are distinct; in every draw some device gets 8 blocks from every device of the other section.
All inputs are finite; a program needn't handle non-finite values.
Results may differ from a plain program's by a relative error of at most 0.0001.
Values sent between devices are 32-bit elements; how exact they have to be, the bound alone decides.
A program may use at most 64 MiB of HBM per device.

v0:
```python
import functools

import jax
import jax.numpy as jnp
from jax import lax
from jax.experimental import pallas as pl
from jax.experimental.pallas import tpu as pltpu
from jax.sharding import PartitionSpec as P

NODES = 64
HALO = 256
LANES = 128
ROWS = 4
DEPTH = 384
PARTS = DEPTH // LANES
STEP = 0.25
MESH = pl.DeviceIdType.MESH
F32 = jnp.float32
BF16 = jnp.bfloat16


def split(value):
    high = value.astype(BF16)
    return high, (value - high.astype(F32)).astype(BF16)


def kernel(
    n,
    links,
    scale,
    donors,
    select,
    fields,
    volume,
    faces,
    patterns,
    choose,
    out,
    table,
    landed,
    first,
    second,
    donated,
    outgoing,
    packed,
    rims,
    operand,
    weights,
    padded,
    own,
    mapped,
    block_send,
    block_recv,
    rim_send,
    rim_recv,
):
    sec, me = lax.axis_index("sec"), lax.axis_index("elem")
    other = 1 - sec
    elements = fields.shape[1]
    slots = donors.shape[1]
    per_device = slots // n
    block = per_device * ROWS
    components = fields.shape[0]
    tail = components - 2 * LANES

    barrier = pltpu.get_barrier_semaphore()
    for j in range(n):
        pl.semaphore_signal(barrier, inc=1, device_id=(other, j), device_id_type=MESH)

    @pl.when(me > 0)
    def _():
        pl.semaphore_signal(barrier, inc=1, device_id=(sec, me - 1), device_id_type=MESH)

    @pl.when(me < n - 1)
    def _():
        pl.semaphore_signal(barrier, inc=1, device_id=(sec, me + 1), device_id_type=MESH)

    for c in range(elements // LANES):
        for j in range(PARTS):
            if j < 2:
                piece = fields[j * LANES : (j + 1) * LANES, c * LANES : (c + 1) * LANES]
            else:
                piece = jnp.concatenate(
                    [
                        fields[2 * LANES : components, c * LANES : (c + 1) * LANES],
                        jnp.zeros((LANES - tail, LANES), F32),
                    ],
                    axis=0,
                )
            table[pl.ds(c * LANES * ROWS + j, LANES, stride=ROWS), :] = jnp.transpose(piece)
        table[pl.ds(c * LANES * ROWS + 3, LANES, stride=ROWS), :] = jnp.zeros((LANES, LANES), F32)

    def prepare_weights():
        padded[...] = jnp.zeros_like(padded)
        for f in range(7):
            padded[0:components, 0:components] = volume[...] if f == 6 else faces[f]
            for k in range(PARTS):
                strip = jnp.transpose(padded[:, k * LANES : (k + 1) * LANES])
                high, low = split(strip)
                weights[f, k * LANES : (k + 1) * LANES, :] = high
                weights[f, DEPTH + k * LANES : DEPTH + (k + 1) * LANES, :] = high
                weights[f, 2 * DEPTH + k * LANES : 2 * DEPTH + (k + 1) * LANES, :] = low

    def rim_copy(stage, side):
        target = me - 1 if side == 0 else me + 1
        return pltpu.make_async_remote_copy(
            src_ref=packed.at[side],
            dst_ref=rims.at[stage, 1 - side],
            send_sem=rim_send.at[stage, side],
            recv_sem=rim_recv.at[stage, 1 - side],
            device_id=(sec, target),
            device_id_type=MESH,
        )

    def to_operand(row, count, parts):
        for k in range(PARTS):
            high, low = split(parts[k])
            operand[pl.ds(row, count), k * LANES : (k + 1) * LANES] = high
            operand[pl.ds(row, count), DEPTH + k * LANES : DEPTH + (k + 1) * LANES] = low
            operand[pl.ds(row, count), 2 * DEPTH + k * LANES : 2 * DEPTH + (k + 1) * LANES] = high

    def face_products(row):
        def body(f, carry):
            y = jnp.dot(
                operand[pl.ds(pl.multiple_of(row, HALO), HALO), :],
                weights[f],
                preferred_element_type=F32,
            )
            for k in range(PARTS):
                mapped[f, pl.ds(row * ROWS + k, HALO, stride=ROWS), :] = y[:, k * LANES : (k + 1) * LANES]
            return carry

        lax.fori_loop(0, 6, body, 0)

    for stage in range(2):
        state = first if stage == 0 else second

        def donate(i, carry):
            for u in range(8):
                b = i * 8 + u
                row = donors[0, b] * ROWS
                donated[pl.ds(pl.multiple_of(b * ROWS, ROWS), ROWS), :] = table[pl.ds(row, ROWS), :]
            return carry

        lax.fori_loop(0, slots // 8, donate, 0)
        values = donated[...]
        kinds = choose[...]
        result = jnp.zeros((slots * ROWS, LANES), F32)
        for p in range(patterns.shape[0]):
            moved = jnp.dot(values, patterns[p], precision=lax.Precision.HIGHEST, preferred_element_type=F32)
            result = jnp.where(kinds == p, moved, result)
        outgoing[...] = result

        if stage == 0:
            heard = n + (me > 0).astype(jnp.int32) + (me < n - 1).astype(jnp.int32)
            pl.semaphore_wait(barrier, heard)

        def block_copy(j):
            return pltpu.make_async_remote_copy(
                src_ref=outgoing.at[pl.ds(pl.multiple_of(j * block, block), block)],
                dst_ref=landed.at[stage, pl.ds(pl.multiple_of(me * block, block), block)],
                send_sem=block_send.at[stage, j],
                recv_sem=block_recv.at[stage, me],
                device_id=(other, j),
                device_id_type=MESH,
            )

        def arrived(j):
            return pltpu.make_async_remote_copy(
                src_ref=outgoing.at[pl.ds(pl.multiple_of(j * block, block), block)],
                dst_ref=landed.at[stage, pl.ds(pl.multiple_of(j * block, block), block)],
                send_sem=block_send.at[stage, j],
                recv_sem=block_recv.at[stage, j],
                device_id=(other, j),
                device_id_type=MESH,
            )

        for j in range(n):
            block_copy(j).start()
        if stage == 0:
            prepare_weights()
        for j in range(n):
            arrived(j).wait_recv()
        table[elements * ROWS :, :] = landed[stage]

        def pick(i, carry):
            for u in range(8):
                g = i * 8 + u
                row = select[0, g] * ROWS
                state[pl.ds(pl.multiple_of(g * ROWS, ROWS), ROWS), :] = table[pl.ds(row, ROWS), :]
            return carry

        def rim_parts(row):
            return [state[pl.ds(row * ROWS + k, HALO, stride=ROWS), :] for k in range(PARTS)]

        for side, begin in ((0, 0), (1, elements - HALO)):
            lax.fori_loop(begin // 8, (begin + HALO) // 8, pick, 0)
            parts = rim_parts(begin)
            packed[side, 0:HALO, :] = parts[0]
            packed[side, HALO : 2 * HALO, :] = parts[1]
            lower, upper = parts[2][: HALO // 2], parts[2][HALO // 2 :]
            packed[side, 2 * HALO :, :] = lower + pltpu.roll(upper, tail, 1)

            @pl.when(me > 0 if side == 0 else me < n - 1)
            def _():
                rim_copy(stage, side).start()

            to_operand(HALO + begin, HALO, parts)
        lax.fori_loop(HALO // 8, (elements - HALO) // 8, pick, 0)
        for c in range(1, elements // HALO - 1):
            to_operand(HALO + c * HALO, HALO, rim_parts(c * HALO))

        def own_products(c, carry):
            row = HALO + c * HALO
            face_products(row)
            y = jnp.dot(
                operand[pl.ds(pl.multiple_of(row, HALO), HALO), :],
                weights[6],
                preferred_element_type=F32,
            )
            for k in range(PARTS):
                own[pl.ds(c * HALO * ROWS + k, HALO, stride=ROWS), :] = y[:, k * LANES : (k + 1) * LANES]
            return carry

        lax.fori_loop(0, elements // HALO, own_products, 0)

        for side in range(2):
            row = 0 if side == 0 else HALO + elements
            inside = me > 0 if side == 0 else me < n - 1

            @pl.when(inside)
            def _():
                rim_copy(stage, 1 - side).wait_recv()
                folded = rims[stage, side, 2 * HALO :, :]
                lane = lax.broadcasted_iota(jnp.int32, folded.shape, 1)
                lower = jnp.where(lane < tail, folded, 0.0)
                upper = jnp.where(lane < tail, pltpu.roll(folded, LANES - tail, 1), 0.0)
                last = jnp.concatenate([lower, upper], axis=0)
                to_operand(row, HALO, [rims[stage, side, 0:HALO, :], rims[stage, side, HALO : 2 * HALO, :], last])
                face_products(row)

            @pl.when(jnp.logical_not(inside))
            def _():
                for f in range(6):
                    mapped[f, row * ROWS : (row + HALO) * ROWS, :] = jnp.zeros((HALO * ROWS, LANES), F32)

        def advance(i, carry):
            for u in range(8):
                g = i * 8 + u
                here = pl.ds(pl.multiple_of(g * ROWS, ROWS), ROWS)
                total = own[here, :]
                for f in range(6):
                    row = links[f, g] * ROWS
                    total = total + mapped[f, pl.ds(row, ROWS), :]
                stepped = state[here, :] + (STEP * scale[0, g]) * total
                if stage == 0:
                    table[here, :] = stepped
                else:
                    table[here, :] = 0.5 * first[here, :] + 0.5 * stepped
            return carry

        lax.fori_loop(0, elements // 8, advance, 0)
        for j in range(n):
            block_copy(j).wait_send()
        for side in range(2):

            @pl.when(me > 0 if side == 0 else me < n - 1)
            def _():
                rim_copy(stage, side).wait_send()

    for c in range(elements // LANES):
        for j in range(PARTS):
            piece = jnp.transpose(table[pl.ds(c * LANES * ROWS + j, LANES, stride=ROWS), :])
            high = min((j + 1) * LANES, components)
            out[j * LANES : high, c * LANES : (c + 1) * LANES] = piece[: high - j * LANES]


def local(
    n,
    fields,
    jacobian,
    face_links,
    volume_matrix,
    face_matrices,
    patterns,
    donor_index,
    pattern_index,
    receivers,
):
    components, elements = fields.shape[1:]
    slots = donor_index.shape[1]
    slot = jnp.arange(slots, dtype=jnp.int32)
    hit = receivers[0][None, :] == jnp.arange(elements, dtype=jnp.int32)[:, None]
    found = jnp.max(jnp.where(hit, slot[None, :], -1), axis=1)
    index = jnp.arange(elements, dtype=jnp.int32)
    select = jnp.where(found >= 0, elements + found, index)[None]
    choose = jnp.broadcast_to(
        jnp.repeat(pattern_index[0], ROWS)[:, None], (slots * ROWS, LANES)
    )
    turned = jnp.transpose(patterns, (0, 2, 1))
    empty = jnp.zeros_like(turned)
    twice = jnp.concatenate(
        [jnp.concatenate([turned, empty], axis=2), jnp.concatenate([empty, turned], axis=2)], axis=1
    )
    smem = pl.BlockSpec(memory_space=pltpu.SMEM)
    vmem = pl.BlockSpec(memory_space=pltpu.VMEM)
    wide = elements + 2 * HALO
    result = pl.pallas_call(
        functools.partial(kernel, n),
        out_shape=jax.ShapeDtypeStruct((components, elements), F32),
        in_specs=[smem] * 4 + [vmem] * 5,
        out_specs=vmem,
        scratch_shapes=[
            pltpu.VMEM(((elements + slots) * ROWS, LANES), F32),
            pltpu.VMEM((2, slots * ROWS, LANES), F32),
            pltpu.VMEM((elements * ROWS, LANES), F32),
            pltpu.VMEM((elements * ROWS, LANES), F32),
            pltpu.VMEM((slots * ROWS, LANES), F32),
            pltpu.VMEM((slots * ROWS, LANES), F32),
            pltpu.VMEM((2, 5 * HALO // 2, LANES), F32),
            pltpu.VMEM((2, 2, 5 * HALO // 2, LANES), F32),
            pltpu.VMEM((wide, 3 * DEPTH), BF16),
            pltpu.VMEM((7, 3 * DEPTH, DEPTH), BF16),
            pltpu.VMEM((DEPTH, DEPTH), F32),
            pltpu.VMEM((elements * ROWS, LANES), F32),
            pltpu.VMEM((6, wide * ROWS, LANES), F32),
            pltpu.SemaphoreType.DMA((2, n)),
            pltpu.SemaphoreType.DMA((2, n)),
            pltpu.SemaphoreType.DMA((2, 2)),
            pltpu.SemaphoreType.DMA((2, 2)),
        ],
        compiler_params=pltpu.CompilerParams(
            collective_id=0, has_side_effects=True, vmem_limit_bytes=62 * 1024 * 1024
        ),
    )(
        face_links[0],
        jacobian,
        donor_index,
        select,
        fields[0],
        volume_matrix[0],
        face_matrices[0],
        twice,
        choose,
    )
    return result[None]


def solution(mesh):
    return jax.shard_map(
        functools.partial(local, mesh.shape["elem"]),
        mesh=mesh,
        in_specs=(
            P("sec", None, "elem"),
            P("sec", "elem"),
            P("sec", None, "elem"),
            P("sec", None, None),
            P("sec", None, None, None),
            P(),
            P("sec", "elem"),
            P("sec", "elem"),
            P("sec", "elem"),
        ),
        out_specs=P("sec", None, "elem"),
        check_vma=False,
    )
```

profile of v0, /device:TPU:21, one launch (start us, length us, event | category | flops | bytes accessed | tf_op | source)
XLA Modules:
  0.0 97.8 jit_solution(18083432481699134596)
XLA Ops:
  0.0 0.9 select_reduce_fusion
  0.9 0.6 reshape_select_fusion.select
  1.5 1.3 %copy.15 = s32[1,6,1024]{2,1,0:T(8,128)} copy(s32[1,6,1024]{2,0,1:T(1,128)} %param.11) | data formatting | bytes 49152
  2.8 0.7 broadcast_in_dim.31
  3.6 0.1 broadcast_in_dim.32
  3.7 1.0 %copy.12 = f32[4,64,64]{1,2,0:T(8,128)S(1)} copy(f32[4,64,64]{2,1,0:T(8,128)} %param.14) | data formatting | bytes 131072 | tf_op args[5]
  4.7 0.8 select_maximum_fusion.patterns
  5.5 0.8 broadcast_in_dim.33.choose
  6.3 88.9 %shard_map.91 = f32[320,1024]{1,0:T(8,128)} custom-call(s32[6,1024]{1,0:T(8,128)} %bitcast.16, f32[1,1024]{1,0:T(1,128)} %scale.1, s32[1,128]{1,0:T(1,128)} %donors.1, s32[1,1024]{1,0:T(1,128)} %reshape_select_fusion.select, f32[320,1024]{1,0:T(8,128)} %bitcast.13, f32[320,320]{1,0:T(8,128)} %bitcast.15, f32[6,320,320]{2,1,0:T(8,128)} %bitcast.12, ...), custom_call_target="tpu_custom_call" | custom-call | tf_op jit(solution)/shard_map/pallas_call | solution.py:308
  95.2 2.5 %copy.17 = f32[1,320,1024]{2,1,0:T(8,128)} copy(f32[1,320,1024]{2,1,0:T(8,128)} %bitcast.11) | data formatting | bytes 2621440
  (2 shorter events, 0.0 us)
where the time goes:
time: 99.7 us; the launch traced here: 97.8 us
  Pallas kernels  88.9 us (89%)
  local copies, waits for them, and re-layouts  6.56 us (7%)
  other arithmetic  2.28 us (2%)
    pallas_call x1, Pallas kernels, local(): pl.pallas_call(functools.partial(kernel, n), out_shape=jax.ShapeDtypeStru...  88.9 us
    unnamed x3, local copies, waits for them, and re-layouts  4.87 us

commit v1 on v0

--- a/solution.py
+++ b/solution.py
@@ -97,9 +97,16 @@
             for k in range(PARTS):
                 strip = jnp.transpose(padded[:, k * LANES : (k + 1) * LANES])
                 high, low = split(strip)
-                weights[f, k * LANES : (k + 1) * LANES, :] = high
-                weights[f, DEPTH + k * LANES : DEPTH + (k + 1) * LANES, :] = high
-                weights[f, 2 * DEPTH + k * LANES : 2 * DEPTH + (k + 1) * LANES, :] = low
+                pair, lanes = f // 2, slice(f % 2 * DEPTH, f % 2 * DEPTH + DEPTH)
+                if k < 2:
+                    places = ((k * LANES, high), ((2 + k) * LANES, high), ((4 + k) * LANES, low))
+                    for row, value in places:
+                        weights[pair, row : row + LANES, lanes] = value
+                else:
+                    ends = (high[:tail], high[:tail], low[:tail], jnp.zeros_like(low[:tail]))
+                    for m, value in enumerate(ends):
+                        row = 6 * LANES + m * tail
+                        weights[pair, row : row + tail, lanes] = value
 
     def rim_copy(stage, side):
         target = me - 1 if side == 0 else me + 1
@@ -113,24 +120,31 @@
         )
 
     def to_operand(row, count, parts):
-        for k in range(PARTS):
+        rows = pl.ds(row, count)
+        for k in range(2):
             high, low = split(parts[k])
-            operand[pl.ds(row, count), k * LANES : (k + 1) * LANES] = high
-            operand[pl.ds(row, count), DEPTH + k * LANES : DEPTH + (k + 1) * LANES] = low
-            operand[pl.ds(row, count), 2 * DEPTH + k * LANES : 2 * DEPTH + (k + 1) * LANES] = high
+            operand[rows, k * LANES : (k + 1) * LANES] = high
+            operand[rows, (2 + k) * LANES : (3 + k) * LANES] = low
+            operand[rows, (4 + k) * LANES : (5 + k) * LANES] = high
+        high, low = split(parts[2])
+        both = high.astype(F32) + pltpu.roll(low.astype(F32), tail, 1)
+        operand[rows, 6 * LANES : 7 * LANES] = both.astype(BF16)
+        operand[rows, 7 * LANES : 8 * LANES] = high
 
     def face_products(row):
-        def body(f, carry):
+        def body(pair, carry):
             y = jnp.dot(
                 operand[pl.ds(pl.multiple_of(row, HALO), HALO), :],
-                weights[f],
+                weights[pair],
                 preferred_element_type=F32,
             )
-            for k in range(PARTS):
-                mapped[f, pl.ds(row * ROWS + k, HALO, stride=ROWS), :] = y[:, k * LANES : (k + 1) * LANES]
-            return carry
-
-        lax.fori_loop(0, 6, body, 0)
+            for half in range(2):
+                for k in range(PARTS):
+                    at = half * DEPTH + k * LANES
+                    mapped[pair * 2 + half, pl.ds(row * ROWS + k, HALO, stride=ROWS), :] = y[:, at : at + LANES]
+            return carry
+
+        lax.fori_loop(0, 3, body, 0)
 
     for stage in range(2):
         state = first if stage == 0 else second
@@ -144,11 +158,24 @@
 
         lax.fori_loop(0, slots // 8, donate, 0)
         values = donated[...]
-        kinds = choose[...]
+        shape = (slots * ROWS, slots)
+        mine = lax.broadcasted_iota(jnp.int32, shape, 0) // ROWS == lax.broadcasted_iota(jnp.int32, shape, 1)
+        kinds = jnp.sum(jnp.where(mine, choose[...].astype(F32), 0.0), axis=1, keepdims=True)
         result = jnp.zeros((slots * ROWS, LANES), F32)
         for p in range(patterns.shape[0]):
-            moved = jnp.dot(values, patterns[p], precision=lax.Precision.HIGHEST, preferred_element_type=F32)
-            result = jnp.where(kinds == p, moved, result)
+            one = patterns[p]
+            none = jnp.zeros_like(one)
+            twice = jnp.concatenate(
+                [jnp.concatenate([one, none], axis=1), jnp.concatenate([none, one], axis=1)], axis=0
+            )
+            moved = lax.dot_general(
+                values,
+                twice,
+                (((1,), (1,)), ((), ())),
+                precision=lax.Precision.HIGHEST,
+                preferred_element_type=F32,
+            )
+            result = jnp.where(kinds == float(p), moved, result)
         outgoing[...] = result
 
         if stage == 0:
@@ -215,7 +242,7 @@
             face_products(row)
             y = jnp.dot(
                 operand[pl.ds(pl.multiple_of(row, HALO), HALO), :],
-                weights[6],
+                weights[3, :, 0:DEPTH],
                 preferred_element_type=F32,
             )
             for k in range(PARTS):
@@ -224,7 +251,7 @@
 
         lax.fori_loop(0, elements // HALO, own_products, 0)
 
-        for side in range(2):
+        for side in (1, 0):
             row = 0 if side == 0 else HALO + elements
             inside = me > 0 if side == 0 else me < n - 1
 
@@ -250,9 +277,9 @@
                 here = pl.ds(pl.multiple_of(g * ROWS, ROWS), ROWS)
                 total = own[here, :]
                 for f in range(6):
-                    row = links[f, g] * ROWS
+                    row = links[f, 0, g] * ROWS
                     total = total + mapped[f, pl.ds(row, ROWS), :]
-                stepped = state[here, :] + (STEP * scale[0, g]) * total
+                stepped = state[here, :] + scale[0, g] * (STEP * total)
                 if stage == 0:
                     table[here, :] = stepped
                 else:
@@ -294,14 +321,6 @@
     found = jnp.max(jnp.where(hit, slot[None, :], -1), axis=1)
     index = jnp.arange(elements, dtype=jnp.int32)
     select = jnp.where(found >= 0, elements + found, index)[None]
-    choose = jnp.broadcast_to(
-        jnp.repeat(pattern_index[0], ROWS)[:, None], (slots * ROWS, LANES)
-    )
-    turned = jnp.transpose(patterns, (0, 2, 1))
-    empty = jnp.zeros_like(turned)
-    twice = jnp.concatenate(
-        [jnp.concatenate([turned, empty], axis=2), jnp.concatenate([empty, turned], axis=2)], axis=1
-    )
     smem = pl.BlockSpec(memory_space=pltpu.SMEM)
     vmem = pl.BlockSpec(memory_space=pltpu.VMEM)
     wide = elements + 2 * HALO
@@ -319,8 +338,8 @@
             pltpu.VMEM((slots * ROWS, LANES), F32),
             pltpu.VMEM((2, 5 * HALO // 2, LANES), F32),
             pltpu.VMEM((2, 2, 5 * HALO // 2, LANES), F32),
-            pltpu.VMEM((wide, 3 * DEPTH), BF16),
-            pltpu.VMEM((7, 3 * DEPTH, DEPTH), BF16),
+            pltpu.VMEM((wide, 8 * LANES), BF16),
+            pltpu.VMEM((4, 8 * LANES, 2 * DEPTH), BF16),
             pltpu.VMEM((DEPTH, DEPTH), F32),
             pltpu.VMEM((elements * ROWS, LANES), F32),
             pltpu.VMEM((6, wide * ROWS, LANES), F32),
@@ -333,15 +352,15 @@
             collective_id=0, has_side_effects=True, vmem_limit_bytes=62 * 1024 * 1024
         ),
     )(
-        face_links[0],
+        jnp.transpose(face_links, (1, 0, 2)),
         jacobian,
         donor_index,
         select,
         fields[0],
         volume_matrix[0],
         face_matrices[0],
-        twice,
-        choose,
+        patterns,
+        pattern_index,
     )
     return result[None]
 

time: 99.7 us -> 88.5 us (0.89); the launches traced: 97.8 us -> 88.3 us
  Pallas kernels: 88.9 us -> 84.3 us
  local copies, waits for them, and re-layouts: 6.56 us -> 2.52 us
    pallas_call x1, Pallas kernels: 88.9 us -> 84.3 us  [local(): pl.pallas_call(functools.partial(kernel, n), out_shape=jax.ShapeDtypeStru...]
    unnamed x3 -> x1, local copies, waits for them, and re-layouts: 4.87 us -> 2.52 us
    broadcast_in_dim x3 -> x0, local copies, waits for them, and re-layouts: 1.69 us -> none  [the longest x2 0.96 us: local(): jnp.broadcast_to(jnp.repeat(pattern_index[0], ROWS)[:, None], (slots * RO...]
where the time goes in v1:
time: 88.5 us; the launch traced here: 88.3 us
  Pallas kernels  84.3 us (95%)
  local copies, waits for them, and re-layouts  2.52 us (3%)
  other arithmetic  1.47 us (2%)
    pallas_call x1, Pallas kernels, local(): pl.pallas_call(functools.partial(kernel, n), out_shape=jax.ShapeDtypeStru...  84.3 us
    unnamed x1, local copies, waits for them, and re-layouts  2.52 us

profile of v1, /device:TPU:21, one launch (start us, length us, event | category | flops | bytes accessed | tf_op | source)
XLA Modules:
  0.0 88.3 jit_solution(17625373561457566911)
XLA Ops:
  0.0 0.9 select_reduce_fusion
  0.9 0.6 reshape_select_fusion.select
  1.5 84.3 %shard_map.91 = f32[320,1024]{1,0:T(8,128)} custom-call(s32[6,1,1024]{2,1,0:T(1,128)} %bitcast.11, f32[1,1024]{1,0:T(1,128)} %scale.1, s32[1,128]{1,0:T(1,128)} %donors.1, s32[1,1024]{1,0:T(1,128)} %reshape_select_fusion.select, f32[320,1024]{1,0:T(8,128)} %bitcast.9, f32[320,320]{1,0:T(8,128)} %bitcast.10, f32[6,320,320]{2,1,0:T(8,128)} %bitcast.8, ...), custom_call_target="tpu_custom_call" | custom-call | tf_op jit(solution)/shard_map/pallas_call | solution.py:327
  85.8 2.5 %copy.11 = f32[1,320,1024]{2,1,0:T(8,128)} copy(f32[1,320,1024]{2,1,0:T(8,128)} %bitcast.7) | data formatting | bytes 2621440
  (2 shorter events, 0.0 us)

commit v2 on v1

--- a/solution.py
+++ b/solution.py
@@ -211,10 +211,9 @@
         table[elements * ROWS :, :] = landed[stage]
 
         def pick(i, carry):
+            group = [table[pl.ds(select[0, i * 8 + u] * ROWS, ROWS), :] for u in range(8)]
             for u in range(8):
-                g = i * 8 + u
-                row = select[0, g] * ROWS
-                state[pl.ds(pl.multiple_of(g * ROWS, ROWS), ROWS), :] = table[pl.ds(row, ROWS), :]
+                state[pl.ds(pl.multiple_of((i * 8 + u) * ROWS, ROWS), ROWS), :] = group[u]
             return carry
 
         def rim_parts(row):
@@ -272,18 +271,18 @@
                     mapped[f, row * ROWS : (row + HALO) * ROWS, :] = jnp.zeros((HALO * ROWS, LANES), F32)
 
         def advance(i, carry):
+            group = []
             for u in range(8):
                 g = i * 8 + u
                 here = pl.ds(pl.multiple_of(g * ROWS, ROWS), ROWS)
-                total = own[here, :]
-                for f in range(6):
-                    row = links[f, 0, g] * ROWS
-                    total = total + mapped[f, pl.ds(row, ROWS), :]
-                stepped = state[here, :] + scale[0, g] * (STEP * total)
-                if stage == 0:
-                    table[here, :] = stepped
-                else:
-                    table[here, :] = 0.5 * first[here, :] + 0.5 * stepped
+                pieces = [mapped[f, pl.ds(links[f, 0, g] * ROWS, ROWS), :] for f in range(6)]
+                total = (pieces[0] + pieces[1]) + (pieces[2] + pieces[3]) + (pieces[4] + pieces[5])
+                stepped = state[here, :] + scale[0, g] * (STEP * (own[here, :] + total))
+                if stage == 1:
+                    stepped = 0.5 * first[here, :] + 0.5 * stepped
+                group.append((here, stepped))
+            for here, stepped in group:
+                table[here, :] = stepped
             return carry
 
         lax.fori_loop(0, elements // 8, advance, 0)

time: 88.5 us -> 88.6 us (level)
  no operation moved by 1% of the time
where the time goes in v2:
time: 88.6 us; the launch traced here: 88.4 us
  Pallas kernels  84.4 us (95%)
  local copies, waits for them, and re-layouts  2.52 us (3%)
  other arithmetic  1.47 us (2%)
    pallas_call x1, Pallas kernels, local(): pl.pallas_call(functools.partial(kernel, n), out_shape=jax.ShapeDtypeStru...  84.4 us
    unnamed x1, local copies, waits for them, and re-layouts  2.52 us

profile of v2, /device:TPU:21, one launch (start us, length us, event | category | flops | bytes accessed | tf_op | source)
XLA Modules:
  0.0 88.4 jit_solution(5974391101172295007)
XLA Ops:
  0.0 0.9 select_reduce_fusion
  0.9 0.6 reshape_select_fusion.select
  1.5 84.4 %shard_map.91 = f32[320,1024]{1,0:T(8,128)} custom-call(s32[6,1,1024]{2,1,0:T(1,128)} %bitcast.11, f32[1,1024]{1,0:T(1,128)} %scale.1, s32[1,128]{1,0:T(1,128)} %donors.1, s32[1,1024]{1,0:T(1,128)} %reshape_select_fusion.select, f32[320,1024]{1,0:T(8,128)} %bitcast.9, f32[320,320]{1,0:T(8,128)} %bitcast.10, f32[6,320,320]{2,1,0:T(8,128)} %bitcast.8, ...), custom_call_target="tpu_custom_call" | custom-call | tf_op jit(solution)/shard_map/pallas_call | solution.py:326
  85.9 2.5 %copy.11 = f32[1,320,1024]{2,1,0:T(8,128)} copy(f32[1,320,1024]{2,1,0:T(8,128)} %bitcast.7) | data formatting | bytes 2621440
  (2 shorter events, 0.0 us)
